TPU v7x, 256 devices: a whole 4x4x8 slice. The times are simulated.
256 devices in a mesh: vox: 64 (over z, x, core), chan: 4 (over y).
Axes of the slice: x: 4, y: 4, z: 8, core: 2. Of those that a mesh axis runs over, the one named last changes fastest.
Arguments:
- model_blocks: bfloat16 [23552, 128, 128], P(('vox', 'chan')), may hold values from -0.15625 to 0.15625
- start_image: float32 [2048, 32, 128], P('vox'), may hold values from 0 to 2
- measured: float32 [2048, 32, 128], P(('vox', 'chan')), may hold values from -6 to 6
- step_size: float32 [32], replicated, may hold values from 0.05 to 0.25
- sent_tiles: int32 [64, 64, 4], P('vox'), may hold values from -1 to 31, as said below
- block_rows: int32 [23552], P(('vox', 'chan')), may hold values from 0 to 7
- block_slots: int32 [23552], P(('vox', 'chan')), may hold values from 0 to 255, as said below
Outputs:
- estimate: float32 [2048, 32, 128], P('vox')
- residual: float32 [2048, 32, 128], P(('vox', 'chan'))
Inputs may be any that keep to these rules, and one draw needn't show every extreme that they name: `sent_tiles`: an entry is -1 for an unused slot, else a tile of slab j; the used slots of one pair (j, v) come first, hold distinct tiles, number 1 to 4, and slab v always uses all 4 slots for itself. `block_slots`: every block names a used slot of its own device's vox index v, that is sent_tiles[j, v, s] is not -1.
All inputs are finite; a program needn't handle non-finite values.
Results may differ from a plain program's by a relative error of at most 0.0045.
Values may be sent and summed in bfloat16 or wider, within the bound.
A program may use at most 64 MiB of HBM per device.

v0:
```python
import jax
import jax.numpy as jnp
from jax import lax
from jax.sharding import PartitionSpec as P

ITERATIONS = 4


def shards(model_blocks, start_image, measured, step_size, sent_tiles, block_rows, block_slots):
    vox_count = lax.axis_size("vox")
    send_table = sent_tiles[0]
    capacity = send_table.shape[1]
    tile_count = start_image.shape[0]
    wave_count = start_image.shape[1]
    block_width = start_image.shape[2]
    row_count = measured.shape[0]
    block_count = model_blocks.shape[0]
    row_hot = (block_rows[None, :] == jnp.arange(row_count, dtype=jnp.int32)[:, None]).astype(
        jnp.float32
    )
    slot_hot = (
        block_slots[None, :] == jnp.arange(vox_count * capacity, dtype=jnp.int32)[:, None]
    ).astype(jnp.float32)
    tile_range = jnp.arange(tile_count, dtype=jnp.int32)[:, None]
    return_hot = (send_table.reshape(1, -1) == tile_range).astype(jnp.float32)
    step_gains = step_size[None, :, None]
    estimate = start_image
    residual = measured
    for iteration in range(ITERATIONS):
        rounded = estimate.astype(jnp.bfloat16)
        outgoing = jnp.take(rounded, jnp.maximum(send_table, 0), axis=0)
        arrived = lax.all_to_all(outgoing, "vox", split_axis=0, concat_axis=0, tiled=True)
        flat_tiles = arrived.reshape(vox_count * capacity, wave_count, block_width)
        forward_picked = jnp.take(flat_tiles, block_slots, axis=0)
        products = jnp.einsum(
            "bwv,bsv->bws", forward_picked, model_blocks, preferred_element_type=jnp.float32
        )
        summed = jnp.dot(
            row_hot,
            products.reshape(block_count, wave_count * block_width),
            precision=lax.Precision.HIGHEST,
        )
        residual = measured - summed.reshape(row_count, wave_count, block_width)
        narrow = residual.astype(jnp.bfloat16)
        picked = jnp.take(narrow, block_rows, axis=0)
        adjoint_terms = jnp.einsum(
            "bws,bsv->bwv", picked, model_blocks, preferred_element_type=jnp.float32
        )
        slot_sums = jnp.dot(
            slot_hot,
            adjoint_terms.reshape(block_count, wave_count * block_width),
            precision=lax.Precision.HIGHEST,
        )
        slot_sums = slot_sums.reshape(vox_count, capacity, wave_count, block_width)
        returned = lax.all_to_all(slot_sums, "vox", split_axis=0, concat_axis=0, tiled=True)
        local_sum = jnp.dot(
            return_hot,
            returned.reshape(-1, wave_count * block_width),
            precision=lax.Precision.HIGHEST,
        )
        slab_total = lax.psum(local_sum, "chan")
        estimate = jnp.maximum(
            estimate + step_gains * slab_total.reshape(tile_count, wave_count, block_width), 0.0
        )
    return (estimate, residual)


def solution(mesh):
    in_specs = (
        P(("vox", "chan"), None, None),
        P("vox", None, None),
        P(("vox", "chan"), None, None),
        P(),
        P("vox", None, None),
        P(("vox", "chan")),
        P(("vox", "chan")),
    )
    out_specs = (P("vox", None, None), P(("vox", "chan"), None, None))
    return jax.shard_map(shards, mesh=mesh, in_specs=in_specs, out_specs=out_specs, check_vma=False)
```

profile of v0, /device:TPU:2, one launch (start us, length us, event | category | flops | bytes accessed | tf_op | source)
XLA Modules:
  0.0 964.7 jit_solution(2402718531708179896)
XLA Ops:
  12.4 2.7 broadcast_select_fusion.3
  15.1 12.3 %all-to-all-start = ((bf16[64,4,32,128]{3,2,1,0:T(8,128)(2,1)}), bf16[64,4,32,128]{3,2,1,0:T(8,128)(2,1)}, u32[]{:S(2)}, u32[]{:S(2)}) async-start(bf16[64,4,32,128]{3,2,1,0:T(8,128)(2,1)} %broadcast_select_fusion.3), calls=%async_computation | async-start | bytes 4194304 | tf_op jit(solution)/shard_map/all_to_all | solution.py:32
  27.6 51.0 %all-to-all-done = bf16[64,4,32,128]{3,2,1,0:T(8,128)(2,1)} async-done(((bf16[64,4,32,128]{3,2,1,0:T(8,128)(2,1)}), bf16[64,4,32,128]{3,2,1,0:T(8,128)(2,1)}, u32[]{:S(2)}, u32[]{:S(2)}) %all-to-all-start) | async-done | bytes 2097184 | tf_op jit(solution)/shard_map/all_to_all | solution.py:32
  78.6 3.1 gather_fusion.1
  81.8 2.8 fusion.79
  90.8 2.6 fusion.18
  93.4 4.4 copy.71
  97.8 6.2 all-to-all-start.1
  104.3 95.7 %all-to-all-done.1 = f32[64,4,32,128]{3,2,1,0:T(8,128)} async-done(((f32[64,4,32,128]{3,2,1,0:T(8,128)}), f32[64,4,32,128]{3,2,1,0:T(8,128)}, u32[]{:S(2)}, u32[]{:S(2)}) %all-to-all-start.1) | async-done | bytes 4194336 | tf_op jit(solution)/shard_map/all_to_all | solution.py:55
  200.0 5.9 fusion.32
  206.8 44.8 %all-reduce.5.cloned.1.call-done = f32[32,32,128]{2,1,0:T(8,128)} async-done(((f32[32,32,128]{2,1,0:T(8,128)}), f32[32,32,128]{2,1,0:T(8,128)}) %all-reduce.5.cloned.1.call-update) | async-done | bytes 524304 | tf_op jit(solution)/shard_map/psum | solution.py:61
  256.9 61.7 %all_to_all.40 = bf16[64,4,32,128]{3,2,1,0:T(8,128)(2,1)} all-to-all(bf16[64,4,32,128]{3,2,1,0:T(8,128)(2,1)S(1)} %broadcast_select_fusion.2), channel_id=1, replica_groups=mesh['vox'=64,'chan'=4] {'vox'}, dimensions={0} | all-to-all | bytes 4194304 | tf_op jit(solution)/shard_map/all_to_all | solution.py:32
  318.6 3.1 gather_fusion.4
  321.8 2.8 fusion.75
  330.0 2.6 fusion.16
  335.1 101.8 %all_to_all.41 = f32[64,4,32,128]{3,2,1,0:T(8,128)S(1)} all-to-all(f32[64,4,32,128]{3,2,1,0:T(8,128)S(1)} %copy.78), channel_id=1, replica_groups=mesh['vox'=64,'chan'=4] {'vox'}, dimensions={0} | all-to-all | bytes 8388608 | tf_op jit(solution)/shard_map/all_to_all | solution.py:55
  436.9 3.9 fusion.35
  441.8 43.9 %all-reduce.7.cloned.1.call-done = f32[32,32,128]{2,1,0:T(8,128)} async-done(((f32[32,32,128]{2,1,0:T(8,128)}), f32[32,32,128]{2,1,0:T(8,128)}) %all-reduce.7.cloned.1.call-update) | async-done | bytes 524304 | tf_op jit(solution)/shard_map/psum | solution.py:61
  492.0 61.8 %all_to_all.42 = bf16[64,4,32,128]{3,2,1,0:T(8,128)(2,1)} all-to-all(bf16[64,4,32,128]{3,2,1,0:T(8,128)(2,1)S(1)} %broadcast_select_fusion.1), channel_id=1, replica_groups=mesh['vox'=64,'chan'=4] {'vox'}, dimensions={0} | all-to-all | bytes 4194304 | tf_op jit(solution)/shard_map/all_to_all | solution.py:32
  553.8 3.1 gather_fusion.7
  557.0 2.8 fusion.71
  565.2 2.6 fusion.14
  570.3 101.6 %all_to_all.43 = f32[64,4,32,128]{3,2,1,0:T(8,128)S(1)} all-to-all(f32[64,4,32,128]{3,2,1,0:T(8,128)S(1)} %copy.85), channel_id=1, replica_groups=mesh['vox'=64,'chan'=4] {'vox'}, dimensions={0} | all-to-all | bytes 8388608 | tf_op jit(solution)/shard_map/all_to_all | solution.py:55
  671.9 3.9 fusion.38
  676.8 43.9 %all-reduce.9.cloned.1.call-done = f32[32,32,128]{2,1,0:T(8,128)} async-done(((f32[32,32,128]{2,1,0:T(8,128)}), f32[32,32,128]{2,1,0:T(8,128)}) %all-reduce.9.cloned.1.call-update) | async-done | bytes 524304 | tf_op jit(solution)/shard_map/psum | solution.py:61
  726.0 61.9 %all_to_all.44 = bf16[64,4,32,128]{3,2,1,0:T(8,128)(2,1)} all-to-all(bf16[64,4,32,128]{3,2,1,0:T(8,128)(2,1)S(1)} %broadcast_select_fusion), channel_id=1, replica_groups=mesh['vox'=64,'chan'=4] {'vox'}, dimensions={0} | all-to-all | bytes 4194304 | tf_op jit(solution)/shard_map/all_to_all | solution.py:32
  787.9 3.1 gather_fusion.10
  791.1 2.8 fusion.67
  799.9 2.6 fusion.12
  805.0 101.7 %all_to_all.45 = f32[64,4,32,128]{3,2,1,0:T(8,128)S(1)} all-to-all(f32[64,4,32,128]{3,2,1,0:T(8,128)S(1)} %copy.92), channel_id=1, replica_groups=mesh['vox'=64,'chan'=4] {'vox'}, dimensions={0} | all-to-all | bytes 8388608 | tf_op jit(solution)/shard_map/all_to_all | solution.py:55
  906.7 3.9 fusion.41
  913.1 42.3 %all-reduce.11.cloned.1.call-done = f32[32,32,128]{2,1,0:T(8,128)} async-done(((f32[32,32,128]{2,1,0:T(8,128)}), f32[32,32,128]{2,1,0:T(8,128)}) %all-reduce.11.cloned.1.call-update) | async-done | bytes 524304 | tf_op jit(solution)/shard_map/psum | solution.py:61
  (81 shorter events, 60.2 us)
Async XLA Ops:
  7.2 74.6 %copy-start = (bf16[92,128,128]{2,1,0:T(8,128)(2,1)S(1)}, bf16[92,128,128]{2,1,0:T(8,128)(2,1)}, u32[]{:S(2)}) copy-start(bf16[92,128,128]{2,1,0:T(8,128)(2,1)} %param.13) | copy-start | bytes 9043972
  15.1 12.4 %copy-start.4 = (s32[92]{0:T(128)S(1)}, s32[92]{0:T(128)}, u32[]{:S(2)}) copy-start(s32[92]{0:T(128)} %param.19) | copy-start | bytes 1108
  15.1 12.4 %copy-start.6 = (s32[92]{0:T(128)S(1)}, s32[92]{0:T(128)}, u32[]{:S(2)}) copy-start(s32[92]{0:T(128)} %param.18) | copy-start | bytes 1108
  15.1 63.5 %all-to-all-start = ((bf16[64,4,32,128]{3,2,1,0:T(8,128)(2,1)}), bf16[64,4,32,128]{3,2,1,0:T(8,128)(2,1)}, u32[]{:S(2)}, u32[]{:S(2)}) async-start(bf16[64,4,32,128]{3,2,1,0:T(8,128)(2,1)} %broadcast_select_fusion.3), calls=%async_computation | async-start | bytes 4194304 | tf_op jit(solution)/shard_map/all_to_all | solution.py:32
  84.6 0.9 copy-start.2
  97.8 6.2 copy-start.3
  97.8 102.1 %all-to-all-start.1 = ((f32[64,4,32,128]{3,2,1,0:T(8,128)}), f32[64,4,32,128]{3,2,1,0:T(8,128)}, u32[]{:S(2)}, u32[]{:S(2)}) async-start(f32[64,4,32,128]{3,2,1,0:T(8,128)} %copy.71), calls=%async_computation.1 | async-start | bytes 8388608 | tf_op jit(solution)/shard_map/all_to_all | solution.py:55
  104.0 147.6 %all-reduce.5.cloned.1.call-start = ((), (), s32[]{:S(2)}) async-start(), calls=%async_computation.8 | async-start | bytes 1048576 | tf_op jit(solution)/shard_map/psum | solution.py:61
  200.0 51.7 %copy-start.5 = (f32[32]{0:T(128)S(1)}, f32[32]{0:T(128)}, u32[]{:S(2)}) copy-start(f32[32]{0:T(128)} %param.16) | copy-start | bytes 388
  206.8 278.9 %all-reduce.7.cloned.1.call-start = ((), (), s32[]{:S(2)}) async-start(), calls=%async_computation.9 | async-start | bytes 1048576 | tf_op jit(solution)/shard_map/psum | solution.py:61
  441.7 278.9 %all-reduce.9.cloned.1.call-start = ((), (), s32[]{:S(2)}) async-start(), calls=%async_computation.10 | async-start | bytes 1048576 | tf_op jit(solution)/shard_map/psum | solution.py:61
  676.8 278.7 %all-reduce.11.cloned.1.call-start = ((), (), s32[]{:S(2)}) async-start(), calls=%async_computation.11 | async-start | bytes 1048576 | tf_op jit(solution)/shard_map/psum | solution.py:61
  910.6 44.8 %copy-start.1 = (f32[32,32,128]{2,1,0:T(8,128)S(1)}, f32[32,32,128]{2,1,0:T(8,128)}, u32[]{:S(2)}) copy-start(f32[32,32,128]{2,1,0:T(8,128)} %get-tuple-element.14) | copy-start | bytes 1572868
Sparse Core Ops, SparseCore 0:
  206.9 44.6 all-reduce.4
  441.8 43.7 all-reduce.6
  676.9 43.7 all-reduce.8
  911.7 43.7 all-reduce.10
where the time goes:
time: 974 us; the launch traced here: 965 us
  blocking collectives  491 us (50%)
  waiting for transfers between devices  322 us (33%)
  matrix products  54.4 us (6%)
  local copies, waits for them, and re-layouts  46.8 us (5%)
  starting transfers between devices  18.7 us (2%)
  other arithmetic  18.1 us (2%)
  between operations  14.6 us (1%)
    all_to_all x3, blocking collectives, shards(): lax.all_to_all(slot_sums, 'vox', split_axis=0, concat_axis=0, tiled=True)  305 us
    all_to_all x3, blocking collectives, shards(): lax.all_to_all(outgoing, 'vox', split_axis=0, concat_axis=0, tiled=True)  185 us
    psum x4, waiting for transfers between devices, shards(): slab_total = lax.psum(local_sum, 'chan')  175 us
    all_to_all x1, waiting for transfers between devices, shards(): lax.all_to_all(slot_sums, 'vox', split_axis=0, concat_axis=0, tiled=True)  95.7 us
    all_to_all x1, waiting for transfers between devices, shards(): lax.all_to_all(outgoing, 'vox', split_axis=0, concat_axis=0, tiled=True)  51 us
  transfers between devices with their start and end apart: 6, of which 6 were waited for; matrix products, arithmetic and copies ran while one was open for 0% of the time, Pallas kernels for 0%

commit v1 on v0

--- a/solution.py
+++ b/solution.py
@@ -58,7 +58,11 @@
             returned.reshape(-1, wave_count * block_width),
             precision=lax.Precision.HIGHEST,
         )
-        slab_total = lax.psum(local_sum, "chan")
+        slab_total = local_sum
+        for hop in (1, 2):
+            slab_total = slab_total + lax.ppermute(
+                slab_total, "chan", [(dev, dev ^ hop) for dev in range(4)]
+            )
         estimate = jnp.maximum(
             estimate + step_gains * slab_total.reshape(tile_count, wave_count, block_width), 0.0
         )

time: 974 us -> 877 us (0.900)
  waiting for transfers between devices: 322 us -> 229 us
  starting transfers between devices: 18.7 us -> 38.4 us
  between operations: 14.6 us -> 1.64 us
    psum x4 -> x0, waiting for transfers between devices: 175 us -> none  [shards(): slab_total = lax.psum(local_sum, 'chan')]
    ppermute x0 -> x8, waiting for transfers between devices: none -> 82.2 us  [shards(): lax.ppermute(slab_total, 'chan', [(dev, dev ^ hop) for dev in range(4)])]
    ppermute x0 -> x8, starting transfers between devices: none -> 19.9 us  [shards(): lax.ppermute(slab_total, 'chan', [(dev, dev ^ hop) for dev in range(4)])]
  transfers between devices with their start and end apart: 6 -> 10, of which waited for: 6 -> 10; matrix products, arithmetic and copies ran while one was open for 0% -> 0% of each run, Pallas kernels for 0% -> 0%
where the time goes in v1:
time: 877 us; the launch traced here: 866 us
  blocking collectives  485 us (55%)
  waiting for transfers between devices  229 us (26%)
  matrix products  53.7 us (6%)
  local copies, waits for them, and re-layouts  44.3 us (5%)
  starting transfers between devices  38.4 us (4%)
  other arithmetic  13.6 us (2%)
    all_to_all x3, blocking collectives, shards(): lax.all_to_all(slot_sums, 'vox', split_axis=0, concat_axis=0, tiled=True)  305 us
    all_to_all x3, blocking collectives, shards(): lax.all_to_all(outgoing, 'vox', split_axis=0, concat_axis=0, tiled=True)  180 us
    all_to_all x1, waiting for transfers between devices, shards(): lax.all_to_all(slot_sums, 'vox', split_axis=0, concat_axis=0, tiled=True)  95.7 us
    ppermute x8, waiting for transfers between devices, shards(): lax.ppermute(slab_total, 'chan', [(dev, dev ^ hop) for dev in range(4)])  82.2 us
    all_to_all x1, waiting for transfers between devices, shards(): lax.all_to_all(outgoing, 'vox', split_axis=0, concat_axis=0, tiled=True)  51 us
    ppermute x8, starting transfers between devices, shards(): lax.ppermute(slab_total, 'chan', [(dev, dev ^ hop) for dev in range(4)])  19.9 us
    dot_general x4, matrix products, shards(): jnp.dot(return_hot, returned.reshape(-1, wave_count * block_width), preci...  17.7 us
  transfers between devices with their start and end apart: 10, of which 10 were waited for; matrix products, arithmetic and copies ran while one was open for 0% of the time, Pallas kernels for 0%

profile of v1, /device:TPU:2, one launch (start us, length us, event | category | flops | bytes accessed | tf_op | source)
XLA Modules:
  0.0 866.1 jit_solution(4559521355233734052)
XLA Ops:
  8.6 12.3 %all-to-all-start = ((bf16[64,4,32,128]{3,2,1,0:T(8,128)(2,1)}), bf16[64,4,32,128]{3,2,1,0:T(8,128)(2,1)}, u32[]{:S(2)}, u32[]{:S(2)}) async-start(bf16[64,4,32,128]{3,2,1,0:T(8,128)(2,1)} %broadcast_select_fusion.3), calls=%async_computation | async-start | bytes 4194304 | tf_op jit(solution)/shard_map/all_to_all | solution.py:32
  21.0 51.0 %all-to-all-done = bf16[64,4,32,128]{3,2,1,0:T(8,128)(2,1)} async-done(((bf16[64,4,32,128]{3,2,1,0:T(8,128)(2,1)}), bf16[64,4,32,128]{3,2,1,0:T(8,128)(2,1)}, u32[]{:S(2)}, u32[]{:S(2)}) %all-to-all-start) | async-done | bytes 2097184 | tf_op jit(solution)/shard_map/all_to_all | solution.py:32
  72.1 3.1 gather_fusion.1
  75.2 2.8 fusion.67
  86.9 4.4 copy.71
  91.3 6.2 all-to-all-start.1
  97.7 95.7 %all-to-all-done.1 = f32[64,4,32,128]{3,2,1,0:T(8,128)} async-done(((f32[64,4,32,128]{3,2,1,0:T(8,128)}), f32[64,4,32,128]{3,2,1,0:T(8,128)}, u32[]{:S(2)}, u32[]{:S(2)}) %all-to-all-start.1) | async-done | bytes 4194336 | tf_op jit(solution)/shard_map/all_to_all | solution.py:55
  193.4 5.9 fusion.9
  201.0 10.0 %collective-permute-done = f32[32,4096]{1,0:T(8,128)S(1)} collective-permute-done((f32[32,4096]{1,0:T(8,128)S(1)}, f32[32,4096]{1,0:T(8,128)S(1)}, u32[]{:S(2)}, u32[]{:S(2)}) %collective-permute-start) | collective-permute-done | bytes 524320 | tf_op jit(solution)/shard_map/ppermute | solution.py:63
  211.1 3.4 collective-permute-start.1
  214.4 10.2 %collective-permute-done.1 = f32[32,4096]{1,0:T(8,128)S(1)} collective-permute-done((f32[32,4096]{1,0:T(8,128)S(1)}, f32[32,4096]{1,0:T(8,128)S(1)}, u32[]{:S(2)}, u32[]{:S(2)}) %collective-permute-start.1) | collective-permute-done | bytes 524320 | tf_op jit(solution)/shard_map/ppermute | solution.py:63
  229.8 60.7 %all_to_all.40 = bf16[64,4,32,128]{3,2,1,0:T(8,128)(2,1)} all-to-all(bf16[64,4,32,128]{3,2,1,0:T(8,128)(2,1)S(1)} %broadcast_select_fusion.2), channel_id=1, replica_groups=mesh['vox'=64,'chan'=4] {'vox'}, dimensions={0} | all-to-all | bytes 4194304 | tf_op jit(solution)/shard_map/all_to_all | solution.py:32
  290.5 3.1 gather_fusion.4
  306.9 101.9 %all_to_all.41 = f32[64,4,32,128]{3,2,1,0:T(8,128)S(1)} all-to-all(f32[64,4,32,128]{3,2,1,0:T(8,128)S(1)} %copy.78), channel_id=1, replica_groups=mesh['vox'=64,'chan'=4] {'vox'}, dimensions={0} | all-to-all | bytes 8388608 | tf_op jit(solution)/shard_map/all_to_all | solution.py:55
  408.8 3.9 fusion.6
  414.4 10.6 %collective-permute-done.2 = f32[32,4096]{1,0:T(8,128)S(1)} collective-permute-done((f32[32,4096]{1,0:T(8,128)S(1)}, f32[32,4096]{1,0:T(8,128)S(1)}, u32[]{:S(2)}, u32[]{:S(2)}) %collective-permute-start.2) | collective-permute-done | bytes 524320 | tf_op jit(solution)/shard_map/ppermute | solution.py:63
  425.0 3.3 collective-permute-start.3
  428.3 10.3 %collective-permute-done.3 = f32[32,4096]{1,0:T(8,128)S(1)} collective-permute-done((f32[32,4096]{1,0:T(8,128)S(1)}, f32[32,4096]{1,0:T(8,128)S(1)}, u32[]{:S(2)}, u32[]{:S(2)}) %collective-permute-start.3) | collective-permute-done | bytes 524320 | tf_op jit(solution)/shard_map/ppermute | solution.py:63
  443.8 59.7 %all_to_all.42 = bf16[64,4,32,128]{3,2,1,0:T(8,128)(2,1)} all-to-all(bf16[64,4,32,128]{3,2,1,0:T(8,128)(2,1)S(1)} %broadcast_select_fusion.1), channel_id=1, replica_groups=mesh['vox'=64,'chan'=4] {'vox'}, dimensions={0} | all-to-all | bytes 4194304 | tf_op jit(solution)/shard_map/all_to_all | solution.py:32
  503.6 3.1 gather_fusion.7
  520.0 101.6 %all_to_all.43 = f32[64,4,32,128]{3,2,1,0:T(8,128)S(1)} all-to-all(f32[64,4,32,128]{3,2,1,0:T(8,128)S(1)} %copy.85), channel_id=1, replica_groups=mesh['vox'=64,'chan'=4] {'vox'}, dimensions={0} | all-to-all | bytes 8388608 | tf_op jit(solution)/shard_map/all_to_all | solution.py:55
  621.6 3.9 fusion.3
  627.2 10.6 %collective-permute-done.4 = f32[32,4096]{1,0:T(8,128)S(1)} collective-permute-done((f32[32,4096]{1,0:T(8,128)S(1)}, f32[32,4096]{1,0:T(8,128)S(1)}, u32[]{:S(2)}, u32[]{:S(2)}) %collective-permute-start.4) | collective-permute-done | bytes 524320 | tf_op jit(solution)/shard_map/ppermute | solution.py:63
  637.9 3.3 collective-permute-start.5
  641.1 10.3 %collective-permute-done.5 = f32[32,4096]{1,0:T(8,128)S(1)} collective-permute-done((f32[32,4096]{1,0:T(8,128)S(1)}, f32[32,4096]{1,0:T(8,128)S(1)}, u32[]{:S(2)}, u32[]{:S(2)}) %collective-permute-start.5) | collective-permute-done | bytes 524320 | tf_op jit(solution)/shard_map/ppermute | solution.py:63
  656.6 59.8 %all_to_all.44 = bf16[64,4,32,128]{3,2,1,0:T(8,128)(2,1)} all-to-all(bf16[64,4,32,128]{3,2,1,0:T(8,128)(2,1)S(1)} %broadcast_select_fusion), channel_id=1, replica_groups=mesh['vox'=64,'chan'=4] {'vox'}, dimensions={0} | all-to-all | bytes 4194304 | tf_op jit(solution)/shard_map/all_to_all | solution.py:32
  716.4 3.1 gather_fusion.10
  732.8 101.7 %all_to_all.45 = f32[64,4,32,128]{3,2,1,0:T(8,128)S(1)} all-to-all(f32[64,4,32,128]{3,2,1,0:T(8,128)S(1)} %copy.92), channel_id=1, replica_groups=mesh['vox'=64,'chan'=4] {'vox'}, dimensions={0} | all-to-all | bytes 8388608 | tf_op jit(solution)/shard_map/all_to_all | solution.py:55
  834.5 3.9 fusion
  840.1 10.6 %collective-permute-done.6 = f32[32,4096]{1,0:T(8,128)S(1)} collective-permute-done((f32[32,4096]{1,0:T(8,128)S(1)}, f32[32,4096]{1,0:T(8,128)S(1)}, u32[]{:S(2)}, u32[]{:S(2)}) %collective-permute-start.6) | collective-permute-done | bytes 524320 | tf_op jit(solution)/shard_map/ppermute | solution.py:63
  850.8 3.3 collective-permute-start.7
  854.7 9.7 %collective-permute-done.7 = f32[32,4096]{1,0:T(8,128)S(1)} collective-permute-done((f32[32,4096]{1,0:T(8,128)S(1)}, f32[32,4096]{1,0:T(8,128)S(1)}, u32[]{:S(2)}, u32[]{:S(2)}) %collective-permute-start.7) | collective-permute-done | bytes 524320 | tf_op jit(solution)/shard_map/ppermute | solution.py:63
  (107 shorter events, 80.8 us)
Async XLA Ops:
  0.6 74.6 %copy-start = (bf16[92,128,128]{2,1,0:T(8,128)(2,1)S(1)}, bf16[92,128,128]{2,1,0:T(8,128)(2,1)}, u32[]{:S(2)}) copy-start(bf16[92,128,128]{2,1,0:T(8,128)(2,1)} %param.13) | copy-start | bytes 9043972
  8.6 12.4 %copy-start.11 = (s32[92]{0:T(128)S(1)}, s32[92]{0:T(128)}, u32[]{:S(2)}) copy-start(s32[92]{0:T(128)} %param.19) | copy-start | bytes 1108
  8.6 12.4 %copy-start.13 = (s32[92]{0:T(128)S(1)}, s32[92]{0:T(128)}, u32[]{:S(2)}) copy-start(s32[92]{0:T(128)} %param.18) | copy-start | bytes 1108
  8.6 63.5 %all-to-all-start = ((bf16[64,4,32,128]{3,2,1,0:T(8,128)(2,1)}), bf16[64,4,32,128]{3,2,1,0:T(8,128)(2,1)}, u32[]{:S(2)}, u32[]{:S(2)}) async-start(bf16[64,4,32,128]{3,2,1,0:T(8,128)(2,1)} %broadcast_select_fusion.3), calls=%async_computation | async-start | bytes 4194304 | tf_op jit(solution)/shard_map/all_to_all | solution.py:32
  78.1 0.9 copy-start.9
  91.3 6.2 copy-start.10
  91.3 102.1 %all-to-all-start.1 = ((f32[64,4,32,128]{3,2,1,0:T(8,128)}), f32[64,4,32,128]{3,2,1,0:T(8,128)}, u32[]{:S(2)}, u32[]{:S(2)}) async-start(f32[64,4,32,128]{3,2,1,0:T(8,128)} %copy.71), calls=%async_computation.1 | async-start | bytes 8388608 | tf_op jit(solution)/shard_map/all_to_all | solution.py:55
  199.3 26.3 %copy-start.3 = (f32[32,32,128]{2,1,0:T(8,128)S(1)}, f32[32,32,128]{2,1,0:T(8,128)}, u32[]{:S(2)}) copy-start(f32[32,32,128]{2,1,0:T(8,128)} %param.14) | copy-start | bytes 1572868
  199.3 26.3 %copy-start.12 = (f32[32]{0:T(128)S(1)}, f32[32]{0:T(128)}, u32[]{:S(2)}) copy-start(f32[32]{0:T(128)} %param.16) | copy-start | bytes 388
  199.3 11.6 %collective-permute-start = (f32[32,4096]{1,0:T(8,128)S(1)}, f32[32,4096]{1,0:T(8,128)S(1)}, u32[]{:S(2)}, u32[]{:S(2)}) collective-permute-start(f32[32,4096]{1,0:T(8,128)S(1)} %fusion.9), channel_id=1, source_target_pairs={{0,1},{1,0},{2,3},{3,2},{4,5},{5,4},{6,7},{7,6},{8,9},{9,8},{10,11... | collective-permute-start | bytes 1572872 | tf_op jit(solution)/shard_map/ppermute | solution.py:63
  211.1 13.6 %collective-permute-start.1 = (f32[32,4096]{1,0:T(8,128)S(1)}, f32[32,4096]{1,0:T(8,128)S(1)}, u32[]{:S(2)}, u32[]{:S(2)}) collective-permute-start(f32[32,4096]{1,0:T(8,128)S(1)} %add.61), channel_id=1, source_target_pairs={{0,2},{1,3},{2,0},{3,1},{4,6},{5,7},{6,4},{7,5},{8,10},{9,11},{10,... | collective-permute-start | bytes 1572872 | tf_op jit(solution)/shard_map/ppermute | solution.py:63
  224.8 0.8 copy-start.7
  412.7 26.1 %copy-start.4 = (f32[32,32,128]{2,1,0:T(8,128)S(1)}, f32[32,32,128]{2,1,0:T(8,128)}, u32[]{:S(2)}) copy-start(f32[32,32,128]{2,1,0:T(8,128)} %param.14) | copy-start | bytes 1572868
  412.7 26.1 %copy-start.8 = (f32[4,8,32,128]{3,2,1,0:T(8,128)S(1)}, f32[4,8,32,128]{3,2,1,0:T(8,128)}, u32[]{:S(2)}) copy-start(f32[4,8,32,128]{3,2,1,0:T(8,128)} %copy-done.7) | copy-start | bytes 1572868
  412.7 12.2 %collective-permute-start.2 = (f32[32,4096]{1,0:T(8,128)S(1)}, f32[32,4096]{1,0:T(8,128)S(1)}, u32[]{:S(2)}, u32[]{:S(2)}) collective-permute-start(f32[32,4096]{1,0:T(8,128)S(1)} %fusion.6), channel_id=1, source_target_pairs={{0,1},{1,0},{2,3},{3,2},{4,5},{5,4},{6,7},{7,6},{8,9},{9,8},{10,11... | collective-permute-start | bytes 1572872 | tf_op jit(solution)/shard_map/ppermute | solution.py:63
  425.0 13.6 %collective-permute-start.3 = (f32[32,4096]{1,0:T(8,128)S(1)}, f32[32,4096]{1,0:T(8,128)S(1)}, u32[]{:S(2)}, u32[]{:S(2)}) collective-permute-start(f32[32,4096]{1,0:T(8,128)S(1)} %add.64), channel_id=1, source_target_pairs={{0,2},{1,3},{2,0},{3,1},{4,6},{5,7},{6,4},{7,5},{8,10},{9,11},{10,... | collective-permute-start | bytes 1572872 | tf_op jit(solution)/shard_map/ppermute | solution.py:63
  625.5 26.9 %copy-start.1 = (f32[32,32,128]{2,1,0:T(8,128)S(1)}, f32[32,32,128]{2,1,0:T(8,128)}, u32[]{:S(2)}) copy-start(f32[32,32,128]{2,1,0:T(8,128)} %get-tuple-element.14) | copy-start | bytes 1572868
  625.6 12.2 %collective-permute-start.4 = (f32[32,4096]{1,0:T(8,128)S(1)}, f32[32,4096]{1,0:T(8,128)S(1)}, u32[]{:S(2)}, u32[]{:S(2)}) collective-permute-start(f32[32,4096]{1,0:T(8,128)S(1)} %fusion.3), channel_id=1, source_target_pairs={{0,1},{1,0},{2,3},{3,2},{4,5},{5,4},{6,7},{7,6},{8,9},{9,8},{10,11... | collective-permute-start | bytes 1572872 | tf_op jit(solution)/shard_map/ppermute | solution.py:63
  637.9 13.6 %collective-permute-start.5 = (f32[32,4096]{1,0:T(8,128)S(1)}, f32[32,4096]{1,0:T(8,128)S(1)}, u32[]{:S(2)}, u32[]{:S(2)}) collective-permute-start(f32[32,4096]{1,0:T(8,128)S(1)} %add.67), channel_id=1, source_target_pairs={{0,2},{1,3},{2,0},{3,1},{4,6},{5,7},{6,4},{7,5},{8,10},{9,11},{10,... | collective-permute-start | bytes 1572872 | tf_op jit(solution)/shard_map/ppermute | solution.py:63
  651.6 0.8 copy-start.5
  838.5 26.1 %copy-start.2 = (f32[32,32,128]{2,1,0:T(8,128)S(1)}, f32[32,32,128]{2,1,0:T(8,128)}, u32[]{:S(2)}) copy-start(f32[32,32,128]{2,1,0:T(8,128)} %get-tuple-element.14) | copy-start | bytes 1572868
  838.5 26.1 %copy-start.6 = (f32[4,8,32,128]{3,2,1,0:T(8,128)S(1)}, f32[4,8,32,128]{3,2,1,0:T(8,128)}, u32[]{:S(2)}) copy-start(f32[4,8,32,128]{3,2,1,0:T(8,128)} %copy-done.5) | copy-start | bytes 1572868
  838.5 12.2 %collective-permute-start.6 = (f32[32,4096]{1,0:T(8,128)S(1)}, f32[32,4096]{1,0:T(8,128)S(1)}, u32[]{:S(2)}, u32[]{:S(2)}) collective-permute-start(f32[32,4096]{1,0:T(8,128)S(1)} %fusion), channel_id=1, source_target_pairs={{0,1},{1,0},{2,3},{3,2},{4,5},{5,4},{6,7},{7,6},{8,9},{9,8},{10,11... | collective-permute-start | bytes 1572872 | tf_op jit(solution)/shard_map/ppermute | solution.py:63
  850.8 13.6 %collective-permute-start.7 = (f32[32,4096]{1,0:T(8,128)S(1)}, f32[32,4096]{1,0:T(8,128)S(1)}, u32[]{:S(2)}, u32[]{:S(2)}) collective-permute-start(f32[32,4096]{1,0:T(8,128)S(1)} %add.70), channel_id=1, source_target_pairs={{0,2},{1,3},{2,0},{3,1},{4,6},{5,7},{6,4},{7,5},{8,10},{9,11},{10,... | collective-permute-start | bytes 1572872 | tf_op jit(solution)/shard_map/ppermute | solution.py:63
